TPU v7x, 512 devices: a whole 4x4x16 slice. The times are simulated.
512 devices in a mesh: slab: 128 (over x, z, core), ctrl: 4 (over y).
Axes of the slice: x: 4, y: 4, z: 16, core: 2. Of those that a mesh axis runs over, the one named last changes fastest.
Arguments:
- face_pressure: float32 [2097152], P(('slab', 'ctrl')), may hold values from 0 to 18
- face_area: float32 [3, 2097152], P(None, ('slab', 'ctrl')), may hold values from -0.00390625 to 0.00390625
- face_center: float32 [3, 2097152], P(None, ('slab', 'ctrl')), may hold values from -6 to 6
- motion: float32 [6], replicated, may hold values from -1 to 1
- inverse_mass: float32 [6], replicated, may hold values from 0.5 to 2
- control_points: float32 [3, 8192], P(None, ('slab', 'ctrl')), may hold values from -4 to 4
- control_modes: float32 [18, 8192], P(None, ('slab', 'ctrl')), may hold values from -0.25 to 0.25
- node_points: float32 [3, 1024, 32, 128], P(None, 'slab', 'ctrl'), may hold values from -5 to 5
- tile_list: int32 [1024, 32, 16], P('slab', 'ctrl'), may hold values from 0 to 63, as said below
- tile_count: int32 [1024, 32], P('slab', 'ctrl'), may hold values from 0 to 16, as said below
Outputs:
- node_shift: float32 [3, 1024, 32, 128], P(None, 'slab', 'ctrl')
- cell_volume: float32 [1024, 32, 128], P('slab', 'ctrl')
- volume_change: float32 [1024, 32, 128], P('slab', 'ctrl')
- new_state: float32 [6], replicated
Inputs may be any that keep to these rules, and one draw needn't show every extreme that they name: `tile_list`: the entries of one line are distinct tile numbers; only the first tile_count entries of a line are live, the others are to be ignored. `tile_count`: every line in the planes x with 3072 <= 8 x < 5120 has 16 live entries; every other line has at most 4.
All inputs are finite; a program needn't handle non-finite values.
Results may differ from a plain program's by a relative error of at most 0.0003.
Values sent between devices are 32-bit elements; how exact they have to be, the bound alone decides.
A program may use at most 64 MiB of HBM per device.

v0:
```python
import jax
import jax.numpy as jnp
from jax import lax
from jax.sharding import PartitionSpec as P

TILE = 128
TIME_STEP = 0.5
RADIUS = 4.0
GRAVITY = (0.0, 0.0, -0.5, 0.0, 0.0, 0.0)


def shifted(value, axis, by):
    devices = lax.axis_size(axis)
    pairs = [(i, i + by) for i in range(devices) if 0 <= i + by < devices]
    return lax.ppermute(value, axis, pairs)


def surface_loads(pressure, area, center):
    pushed = pressure[None, :] * area
    forces = jnp.sum(pushed, axis=1)
    moment_x = jnp.sum(center[1] * pushed[2] - center[2] * pushed[1])
    moment_y = jnp.sum(center[2] * pushed[0] - center[0] * pushed[2])
    moment_z = jnp.sum(center[0] * pushed[1] - center[1] * pushed[0])
    return jnp.concatenate([forces, jnp.stack([moment_x, moment_y, moment_z])])


def advance(total_loads, motion, inverse_mass):
    acceleration = inverse_mass * total_loads + jnp.array(GRAVITY, dtype=jnp.float32)
    new_state = motion + TIME_STEP * acceleration
    rigid_step = TIME_STEP * motion + 0.5 * TIME_STEP * TIME_STEP * acceleration
    return (new_state, rigid_step)


def mode_mix(rigid_step, modes):
    shaped = modes.reshape(6, 3, modes.shape[1])
    return jnp.einsum("k,kcj->cj", rigid_step, shaped, precision=lax.Precision.HIGHEST)


def kernel_sum(points, tile_ids, counts, center_tiles, coeff_tiles):
    longest = jnp.max(counts)

    def accumulate(entry_id, running):
        picked = jnp.take(tile_ids, entry_id, axis=1)
        centers = jnp.take(center_tiles, picked, axis=1)
        coeffs = jnp.take(coeff_tiles, picked, axis=1)
        square = jnp.zeros((points.shape[1], points.shape[2], centers.shape[2]), jnp.float32)
        for axis_id in range(3):
            offset = points[axis_id][:, :, None] - centers[axis_id][:, None, :]
            square = square + offset * offset
        radial = jnp.sqrt(square) / RADIUS
        falloff = jnp.maximum(1.0 - radial, 0.0)
        fourth = falloff * falloff
        fourth = fourth * fourth
        kernel = fourth * (4.0 * radial + 1.0)
        alive_mask = (entry_id < counts)[:, None, None]
        kernel = jnp.where(alive_mask, kernel, 0.0)
        return running + jnp.einsum("lnj,clj->cln", kernel, coeffs, precision=lax.Precision.HIGHEST)

    start = jnp.zeros((3, points.shape[1], points.shape[2]), jnp.float32)
    return lax.fori_loop(0, longest, accumulate, start)


def cell_volumes(lattice):
    span_x = lattice.shape[-3] - 1
    span_y = lattice.shape[-2] - 1
    corners = {}
    for shift_x in range(2):
        for shift_y in range(2):
            for shift_z in range(2):
                sliced = lattice[..., shift_x : shift_x + span_x, shift_y : shift_y + span_y, :]
                if shift_z == 1:
                    sliced = jnp.concatenate(
                        [sliced[..., 1:], jnp.zeros_like(sliced[..., :1])], axis=-1
                    )
                corners[shift_x, shift_y, shift_z] = sliced
    edge_x = 0.0
    edge_y = 0.0
    edge_z = 0.0
    for first in range(2):
        for second in range(2):
            edge_x = edge_x + corners[1, first, second] - corners[0, first, second]
            edge_y = edge_y + corners[first, 1, second] - corners[first, 0, second]
            edge_z = edge_z + corners[first, second, 1] - corners[first, second, 0]
    edge_x = 0.25 * edge_x
    edge_y = 0.25 * edge_y
    edge_z = 0.25 * edge_z
    ex0, ex1, ex2 = (edge_x[..., 0, :, :, :], edge_x[..., 1, :, :, :], edge_x[..., 2, :, :, :])
    ey0, ey1, ey2 = (edge_y[..., 0, :, :, :], edge_y[..., 1, :, :, :], edge_y[..., 2, :, :, :])
    ez0, ez1, ez2 = (edge_z[..., 0, :, :, :], edge_z[..., 1, :, :, :], edge_z[..., 2, :, :, :])
    return (
        ex0 * (ey1 * ez2 - ey2 * ez1)
        + ex1 * (ey2 * ez0 - ey0 * ez2)
        + ex2 * (ey0 * ez1 - ey1 * ez0)
    )


def local(
    face_pressure,
    face_area,
    face_center,
    motion,
    inverse_mass,
    control_points,
    control_modes,
    node_points,
    tile_list,
    tile_count,
):
    local_loads = surface_loads(face_pressure, face_area, face_center)
    centers_all, modes_all = (
        lax.all_gather(control_points, ("slab", "ctrl"), axis=1, tiled=True),
        lax.all_gather(control_modes, ("slab", "ctrl"), axis=1, tiled=True),
    )
    total_loads = lax.psum(local_loads, ("slab", "ctrl"))
    new_state, rigid_step = advance(total_loads, motion, inverse_mass)
    coeffs_all = mode_mix(rigid_step, modes_all)
    center_tiles = centers_all.reshape(3, -1, TILE)
    coeff_tiles = coeffs_all.reshape(3, -1, TILE)
    plane_count = node_points.shape[1]
    row_count = node_points.shape[2]
    line_nodes = node_points.shape[3]
    slots = tile_list.shape[2]
    node_shift = kernel_sum(
        node_points.reshape(3, -1, line_nodes),
        tile_list.reshape(-1, slots),
        tile_count.reshape(-1),
        center_tiles,
        coeff_tiles,
    ).reshape(node_points.shape)
    displaced = node_points + node_shift
    stacked = jnp.stack([node_points, displaced])
    next_plane = shifted(stacked[:, :, :1], "slab", -1)
    widened = jnp.concatenate([stacked, next_plane], axis=2)
    next_row = shifted(widened[:, :, :, :1], "ctrl", -1)
    extended = jnp.concatenate([widened, next_row], axis=3)
    volumes = cell_volumes(extended)
    plane_total = plane_count * lax.axis_size("slab")
    row_total = row_count * lax.axis_size("ctrl")
    plane_ids = lax.axis_index("slab") * plane_count + jnp.arange(plane_count, dtype=jnp.int32)
    row_ids = lax.axis_index("ctrl") * row_count + jnp.arange(row_count, dtype=jnp.int32)
    depth_ids = jnp.arange(line_nodes, dtype=jnp.int32)
    inside = (plane_ids < plane_total - 1)[:, None, None]
    inside = inside & (row_ids < row_total - 1)[None, :, None]
    inside = inside & (depth_ids < line_nodes - 1)[None, None, :]
    volumes = jnp.where(inside[None], volumes, 0.0)
    return (node_shift, volumes[1], volumes[1] - volumes[0], new_state)


def solution(mesh):
    placed = (
        P(("slab", "ctrl")),
        P(None, ("slab", "ctrl")),
        P(None, ("slab", "ctrl")),
        P(),
        P(),
        P(None, ("slab", "ctrl")),
        P(None, ("slab", "ctrl")),
        P(None, "slab", "ctrl", None),
        P("slab", "ctrl", None),
        P("slab", "ctrl"),
    )
    return jax.shard_map(
        local,
        mesh=mesh,
        in_specs=placed,
        out_specs=(
            P(None, "slab", "ctrl", None),
            P("slab", "ctrl", None),
            P("slab", "ctrl", None),
            P(),
        ),
        check_vma=False,
    )
```

profile of v0, /device:TPU:4, one launch (start us, length us, event | category | flops | bytes accessed | tf_op | source)
XLA Modules:
  0.0 821.4 jit_solution(15603495582386284360)
XLA Ops:
  0.6 1.0 fusion.60
  1.6 1.7 subtract_reduce_fusion.2
  3.3 2.0 pad_maximum_fusion.4
  5.3 108.6 %psum.7 = f32[6]{0:T(128)S(1)} all-reduce(f32[6]{0:T(128)S(1)} %pad_maximum_fusion.4), channel_id=1, replica_groups=mesh['slab'=128,'ctrl'=4] {'slab','ctrl'}, use_global_device_ids=true, to_apply=%region_5.0 | all-reduce | flops 6 | bytes 48 | tf_op jit(solution)/shard_map/psum | solution.py:114
  113.9 250.8 %all_gather.6 = f32[18,8192]{0,1:T(8,128)} all-gather(f32[18,16]{0,1:T(8,128)} %param.21), channel_id=1, replica_groups=mesh['slab'=128,'ctrl'=4] {'slab','ctrl'}, dimensions={1}, use_global_device_ids=true | all-gather | bytes 590976 | tf_op jit(solution)/shard_map/all_gather | solution.py:112
  364.8 2.9 copy.23
  368.4 1.1 fusion.43
  369.6 229.6 %all-gather = f32[512,16,3]{1,2,0:T(4,128)S(1)} all-gather(f32[1,16,3]{1,2,0:T(4,128)S(1)} %bitcast.94), channel_id=1, replica_groups=mesh['slab'=128,'ctrl'=4] {'slab','ctrl'}, dimensions={0}, use_global_device_ids=true | all-gather | bytes 98496 | tf_op jit(solution)/shard_map/all_gather | solution.py:111
  600.5 207.5 %while.13 = (s32[]{:T(128)}, f32[3,64,128]{2,0,1:T(4,128)S(1)}, s32[]{:T(128)}, s32[64,16]{0,1:T(8,128)S(1)}, f32[3,64,128]{2,0,1:T(4,128)S(1)}, /*index=5*/s32[...) while((s32[]{:T(128)}, f32[3,64,128]{2,0,1:T(4,128)S(1)}, ...), condition=%wide.region_7.9_spmd, body=%wide.region_6.8_spmd.sunk | while | flops 54601224 | bytes 1480693 | solution.py:60
  601.2 0.7 gather_fusion
  602.7 10.6 %fusion.70 = f32[3,64,128]{2,0,1:T(4,128)S(1)} fusion(f32[3,64,128]{2,0,1:T(4,128)S(1)} %get-tuple-element.258, f32[64,128]{1,0:T(8,128)S(1)} %bitcast.91, f32[64,128]{1,0:T(8,128)S(1)} %get-tuple-element.239, f32[64,128]{1,0:T(8,128)S(1)} %bitcast.92, f32[64,128]{1,0:T(8,128)S(1)} %get-tuple-element.241, f32[64,128]{1,0:T(8,128)S(1)} %bitcast.90, ...), kind=kOutput, calls=%fused_computation.31.clone.1 | convolution fusion | flops 54575104 | bytes 491648 | tf_op jit(solution)/shard_map/while/body/lnj,clj->cln/dot_general | solution.py:57
  614.1 0.7 gather_fusion
  615.0 0.7 gather_fusion.1
  615.7 10.6 %fusion.70 = f32[3,64,128]{2,0,1:T(4,128)S(1)} fusion(f32[3,64,128]{2,0,1:T(4,128)S(1)} %get-tuple-element.258, f32[64,128]{1,0:T(8,128)S(1)} %bitcast.91, f32[64,128]{1,0:T(8,128)S(1)} %get-tuple-element.239, f32[64,128]{1,0:T(8,128)S(1)} %bitcast.92, f32[64,128]{1,0:T(8,128)S(1)} %get-tuple-element.241, f32[64,128]{1,0:T(8,128)S(1)} %bitcast.90, ...), kind=kOutput, calls=%fused_computation.31.clone.1 | convolution fusion | flops 54575104 | bytes 491648 | tf_op jit(solution)/shard_map/while/body/lnj,clj->cln/dot_general | solution.py:57
  627.1 0.7 gather_fusion
  627.9 0.7 gather_fusion.1
  628.6 10.6 %fusion.70 = f32[3,64,128]{2,0,1:T(4,128)S(1)} fusion(f32[3,64,128]{2,0,1:T(4,128)S(1)} %get-tuple-element.258, f32[64,128]{1,0:T(8,128)S(1)} %bitcast.91, f32[64,128]{1,0:T(8,128)S(1)} %get-tuple-element.239, f32[64,128]{1,0:T(8,128)S(1)} %bitcast.92, f32[64,128]{1,0:T(8,128)S(1)} %get-tuple-element.241, f32[64,128]{1,0:T(8,128)S(1)} %bitcast.90, ...), kind=kOutput, calls=%fused_computation.31.clone.1 | convolution fusion | flops 54575104 | bytes 491648 | tf_op jit(solution)/shard_map/while/body/lnj,clj->cln/dot_general | solution.py:57
  640.0 0.7 gather_fusion
  640.9 0.7 gather_fusion.1
  641.5 10.6 %fusion.70 = f32[3,64,128]{2,0,1:T(4,128)S(1)} fusion(f32[3,64,128]{2,0,1:T(4,128)S(1)} %get-tuple-element.258, f32[64,128]{1,0:T(8,128)S(1)} %bitcast.91, f32[64,128]{1,0:T(8,128)S(1)} %get-tuple-element.239, f32[64,128]{1,0:T(8,128)S(1)} %bitcast.92, f32[64,128]{1,0:T(8,128)S(1)} %get-tuple-element.241, f32[64,128]{1,0:T(8,128)S(1)} %bitcast.90, ...), kind=kOutput, calls=%fused_computation.31.clone.1 | convolution fusion | flops 54575104 | bytes 491648 | tf_op jit(solution)/shard_map/while/body/lnj,clj->cln/dot_general | solution.py:57
  653.8 0.7 gather_fusion.1
  654.5 10.6 %fusion.70 = f32[3,64,128]{2,0,1:T(4,128)S(1)} fusion(f32[3,64,128]{2,0,1:T(4,128)S(1)} %get-tuple-element.258, f32[64,128]{1,0:T(8,128)S(1)} %bitcast.91, f32[64,128]{1,0:T(8,128)S(1)} %get-tuple-element.239, f32[64,128]{1,0:T(8,128)S(1)} %bitcast.92, f32[64,128]{1,0:T(8,128)S(1)} %get-tuple-element.241, f32[64,128]{1,0:T(8,128)S(1)} %bitcast.90, ...), kind=kOutput, calls=%fused_computation.31.clone.1 | convolution fusion | flops 54575104 | bytes 491648 | tf_op jit(solution)/shard_map/while/body/lnj,clj->cln/dot_general | solution.py:57
  665.9 0.7 gather_fusion
  666.7 0.7 gather_fusion.1
  667.4 10.6 %fusion.70 = f32[3,64,128]{2,0,1:T(4,128)S(1)} fusion(f32[3,64,128]{2,0,1:T(4,128)S(1)} %get-tuple-element.258, f32[64,128]{1,0:T(8,128)S(1)} %bitcast.91, f32[64,128]{1,0:T(8,128)S(1)} %get-tuple-element.239, f32[64,128]{1,0:T(8,128)S(1)} %bitcast.92, f32[64,128]{1,0:T(8,128)S(1)} %get-tuple-element.241, f32[64,128]{1,0:T(8,128)S(1)} %bitcast.90, ...), kind=kOutput, calls=%fused_computation.31.clone.1 | convolution fusion | flops 54575104 | bytes 491648 | tf_op jit(solution)/shard_map/while/body/lnj,clj->cln/dot_general | solution.py:57
  678.8 0.7 gather_fusion
  680.3 10.6 %fusion.70 = f32[3,64,128]{2,0,1:T(4,128)S(1)} fusion(f32[3,64,128]{2,0,1:T(4,128)S(1)} %get-tuple-element.258, f32[64,128]{1,0:T(8,128)S(1)} %bitcast.91, f32[64,128]{1,0:T(8,128)S(1)} %get-tuple-element.239, f32[64,128]{1,0:T(8,128)S(1)} %bitcast.92, f32[64,128]{1,0:T(8,128)S(1)} %get-tuple-element.241, f32[64,128]{1,0:T(8,128)S(1)} %bitcast.90, ...), kind=kOutput, calls=%fused_computation.31.clone.1 | convolution fusion | flops 54575104 | bytes 491648 | tf_op jit(solution)/shard_map/while/body/lnj,clj->cln/dot_general | solution.py:57
  693.3 10.6 %fusion.70 = f32[3,64,128]{2,0,1:T(4,128)S(1)} fusion(f32[3,64,128]{2,0,1:T(4,128)S(1)} %get-tuple-element.258, f32[64,128]{1,0:T(8,128)S(1)} %bitcast.91, f32[64,128]{1,0:T(8,128)S(1)} %get-tuple-element.239, f32[64,128]{1,0:T(8,128)S(1)} %bitcast.92, f32[64,128]{1,0:T(8,128)S(1)} %get-tuple-element.241, f32[64,128]{1,0:T(8,128)S(1)} %bitcast.90, ...), kind=kOutput, calls=%fused_computation.31.clone.1 | convolution fusion | flops 54575104 | bytes 491648 | tf_op jit(solution)/shard_map/while/body/lnj,clj->cln/dot_general | solution.py:57
  706.2 10.6 %fusion.70 = f32[3,64,128]{2,0,1:T(4,128)S(1)} fusion(f32[3,64,128]{2,0,1:T(4,128)S(1)} %get-tuple-element.258, f32[64,128]{1,0:T(8,128)S(1)} %bitcast.91, f32[64,128]{1,0:T(8,128)S(1)} %get-tuple-element.239, f32[64,128]{1,0:T(8,128)S(1)} %bitcast.92, f32[64,128]{1,0:T(8,128)S(1)} %get-tuple-element.241, f32[64,128]{1,0:T(8,128)S(1)} %bitcast.90, ...), kind=kOutput, calls=%fused_computation.31.clone.1 | convolution fusion | flops 54575104 | bytes 491648 | tf_op jit(solution)/shard_map/while/body/lnj,clj->cln/dot_general | solution.py:57
  717.6 0.7 gather_fusion
  718.5 0.7 gather_fusion.1
  719.1 10.6 %fusion.70 = f32[3,64,128]{2,0,1:T(4,128)S(1)} fusion(f32[3,64,128]{2,0,1:T(4,128)S(1)} %get-tuple-element.258, f32[64,128]{1,0:T(8,128)S(1)} %bitcast.91, f32[64,128]{1,0:T(8,128)S(1)} %get-tuple-element.239, f32[64,128]{1,0:T(8,128)S(1)} %bitcast.92, f32[64,128]{1,0:T(8,128)S(1)} %get-tuple-element.241, f32[64,128]{1,0:T(8,128)S(1)} %bitcast.90, ...), kind=kOutput, calls=%fused_computation.31.clone.1 | convolution fusion | flops 54575104 | bytes 491648 | tf_op jit(solution)/shard_map/while/body/lnj,clj->cln/dot_general | solution.py:57
  732.1 10.6 %fusion.70 = f32[3,64,128]{2,0,1:T(4,128)S(1)} fusion(f32[3,64,128]{2,0,1:T(4,128)S(1)} %get-tuple-element.258, f32[64,128]{1,0:T(8,128)S(1)} %bitcast.91, f32[64,128]{1,0:T(8,128)S(1)} %get-tuple-element.239, f32[64,128]{1,0:T(8,128)S(1)} %bitcast.92, f32[64,128]{1,0:T(8,128)S(1)} %get-tuple-element.241, f32[64,128]{1,0:T(8,128)S(1)} %bitcast.90, ...), kind=kOutput, calls=%fused_computation.31.clone.1 | convolution fusion | flops 54575104 | bytes 491648 | tf_op jit(solution)/shard_map/while/body/lnj,clj->cln/dot_general | solution.py:57
  743.4 0.7 gather_fusion
  744.3 0.7 gather_fusion.1
  745.0 10.6 %fusion.70 = f32[3,64,128]{2,0,1:T(4,128)S(1)} fusion(f32[3,64,128]{2,0,1:T(4,128)S(1)} %get-tuple-element.258, f32[64,128]{1,0:T(8,128)S(1)} %bitcast.91, f32[64,128]{1,0:T(8,128)S(1)} %get-tuple-element.239, f32[64,128]{1,0:T(8,128)S(1)} %bitcast.92, f32[64,128]{1,0:T(8,128)S(1)} %get-tuple-element.241, f32[64,128]{1,0:T(8,128)S(1)} %bitcast.90, ...), kind=kOutput, calls=%fused_computation.31.clone.1 | convolution fusion | flops 54575104 | bytes 491648 | tf_op jit(solution)/shard_map/while/body/lnj,clj->cln/dot_general | solution.py:57
  756.4 0.7 gather_fusion
  757.2 0.7 gather_fusion.1
  757.9 10.6 %fusion.70 = f32[3,64,128]{2,0,1:T(4,128)S(1)} fusion(f32[3,64,128]{2,0,1:T(4,128)S(1)} %get-tuple-element.258, f32[64,128]{1,0:T(8,128)S(1)} %bitcast.91, f32[64,128]{1,0:T(8,128)S(1)} %get-tuple-element.239, f32[64,128]{1,0:T(8,128)S(1)} %bitcast.92, f32[64,128]{1,0:T(8,128)S(1)} %get-tuple-element.241, f32[64,128]{1,0:T(8,128)S(1)} %bitcast.90, ...), kind=kOutput, calls=%fused_computation.31.clone.1 | convolution fusion | flops 54575104 | bytes 491648 | tf_op jit(solution)/shard_map/while/body/lnj,clj->cln/dot_general | solution.py:57
  770.9 10.6 %fusion.70 = f32[3,64,128]{2,0,1:T(4,128)S(1)} fusion(f32[3,64,128]{2,0,1:T(4,128)S(1)} %get-tuple-element.258, f32[64,128]{1,0:T(8,128)S(1)} %bitcast.91, f32[64,128]{1,0:T(8,128)S(1)} %get-tuple-element.239, f32[64,128]{1,0:T(8,128)S(1)} %bitcast.92, f32[64,128]{1,0:T(8,128)S(1)} %get-tuple-element.241, f32[64,128]{1,0:T(8,128)S(1)} %bitcast.90, ...), kind=kOutput, calls=%fused_computation.31.clone.1 | convolution fusion | flops 54575104 | bytes 491648 | tf_op jit(solution)/shard_map/while/body/lnj,clj->cln/dot_general | solution.py:57
  782.2 0.7 gather_fusion
  783.1 0.7 gather_fusion.1
  783.8 10.6 %fusion.70 = f32[3,64,128]{2,0,1:T(4,128)S(1)} fusion(f32[3,64,128]{2,0,1:T(4,128)S(1)} %get-tuple-element.258, f32[64,128]{1,0:T(8,128)S(1)} %bitcast.91, f32[64,128]{1,0:T(8,128)S(1)} %get-tuple-element.239, f32[64,128]{1,0:T(8,128)S(1)} %bitcast.92, f32[64,128]{1,0:T(8,128)S(1)} %get-tuple-element.241, f32[64,128]{1,0:T(8,128)S(1)} %bitcast.90, ...), kind=kOutput, calls=%fused_computation.31.clone.1 | convolution fusion | flops 54575104 | bytes 491648 | tf_op jit(solution)/shard_map/while/body/lnj,clj->cln/dot_general | solution.py:57
  796.7 10.6 %fusion.70 = f32[3,64,128]{2,0,1:T(4,128)S(1)} fusion(f32[3,64,128]{2,0,1:T(4,128)S(1)} %get-tuple-element.258, f32[64,128]{1,0:T(8,128)S(1)} %bitcast.91, f32[64,128]{1,0:T(8,128)S(1)} %get-tuple-element.239, f32[64,128]{1,0:T(8,128)S(1)} %bitcast.92, f32[64,128]{1,0:T(8,128)S(1)} %get-tuple-element.241, f32[64,128]{1,0:T(8,128)S(1)} %bitcast.90, ...), kind=kOutput, calls=%fused_computation.31.clone.1 | convolution fusion | flops 54575104 | bytes 491648 | tf_op jit(solution)/shard_map/while/body/lnj,clj->cln/dot_general | solution.py:57
  808.7 4.3 collective-permute-start
  813.8 0.7 collective-permute-done
  814.5 1.3 collective-permute-start.1
  815.9 4.3 collective-permute-done.1
  (133 shorter events, 17.2 us)
Async XLA Ops:
  364.7 3.7 copy-start.3
  364.7 3.7 copy-start.4
  364.7 3.7 copy-start.5
  364.7 4.9 copy-start.6
  367.6 232.0 %copy-start.1 = (s32[8,8,16]{2,1,0:T(8,128)S(1)}, s32[8,8,16]{2,1,0:T(8,128)}, u32[]{:S(2)}) copy-start(s32[8,8,16]{2,1,0:T(8,128)} %param.23) | copy-start | bytes 12292
  367.6 232.1 %copy-start.2 = (s32[8,8]{1,0:T(8,128)S(1)}, s32[8,8]{1,0:T(8,128)}, u32[]{:S(2)}) copy-start(s32[8,8]{1,0:T(8,128)} %param.24) | copy-start | bytes 772
  367.7 232.8 %copy-start = (f32[3,8,8,128]{3,2,1,0:T(8,128)S(1)}, f32[3,8,8,128]{3,2,1,0:T(8,128)}, u32[]{:S(2)}) copy-start(f32[3,8,8,128]{3,2,1,0:T(8,128)} %param.22) | copy-start | bytes 294916
  808.7 5.8 collective-permute-start
  814.5 5.8 collective-permute-start.1
where the time goes:
time: 822 us; the launch traced here: 821 us
  blocking collectives  589 us (72%)
  matrix products  171 us (21%)
  local copies, waits for them, and re-layouts  26.9 us (3%)
  loops' own time  12.4 us (2%)
  other arithmetic  10.3 us (1%)
    all_gather x1, blocking collectives, local(): lax.all_gather(control_modes, ('slab', 'ctrl'), axis=1, tiled=True)  251 us
    all_gather x1, blocking collectives, local(): lax.all_gather(control_points, ('slab', 'ctrl'), axis=1, tiled=True)  230 us
    dot_general x16, matrix products, accumulate(): jnp.einsum('lnj,clj->cln', kernel, coeffs, precision=lax.Precision.HIGHEST)  170 us
    psum x1, blocking collectives, local(): total_loads = lax.psum(local_loads, ('slab', 'ctrl'))  109 us
  transfers between devices with their start and end apart: 2, of which 2 were waited for; matrix products, arithmetic and copies ran while one was open for 0% of the time, Pallas kernels for 0%

commit v1 on v0

--- a/solution.py
+++ b/solution.py
@@ -109,7 +109,12 @@
     local_loads = surface_loads(face_pressure, face_area, face_center)
     centers_all, modes_all = (
         lax.all_gather(control_points, ("slab", "ctrl"), axis=1, tiled=True),
-        lax.all_gather(control_modes, ("slab", "ctrl"), axis=1, tiled=True),
+        jnp.concatenate(
+            lax.all_to_all(
+                jnp.stack([control_modes] * lax.axis_size(("slab", "ctrl"))), ("slab", "ctrl"), 0, 0
+            ),
+            axis=1,
+        ),
     )
     total_loads = lax.psum(local_loads, ("slab", "ctrl"))
     new_state, rigid_step = advance(total_loads, motion, inverse_mass)

time: 822 us -> 620 us (0.75)
  blocking collectives: 589 us -> 337 us
  local copies, waits for them, and re-layouts: 26.9 us -> 52.4 us
  starting transfers between devices: 5.56 us -> 28.9 us
    all_gather x1 -> x0, blocking collectives: 251 us -> none  [local(): lax.all_gather(control_modes, ('slab', 'ctrl'), axis=1, tiled=True)]
    all_to_all x0 -> x1, starting transfers between devices: none -> 23.3 us  [local(): lax.all_to_all(jnp.stack([control_modes] * lax.axis_size(('slab', 'ctrl')...]
    unnamed x15 -> x26, local copies, waits for them, and re-layouts: 0.48 us -> 12.9 us
    reshape x1 -> x2, local copies, waits for them, and re-layouts: 0.27 us -> 11.1 us  [local(): jnp.concatenate(lax.all_to_all(jnp.stack([control_modes] * lax.axis_size(...]
  transfers between devices with their start and end apart: 2 -> 3, of which waited for: 2 -> 2; matrix products, arithmetic and copies ran while one was open for 0% -> 1% of each run, Pallas kernels for 0% -> 0%
where the time goes in v1:
time: 620 us; the launch traced here: 619 us
  blocking collectives  337 us (54%)
  matrix products  171 us (28%)
  local copies, waits for them, and re-layouts  52.4 us (8%)
  starting transfers between devices  28.9 us (5%)
  loops' own time  12.4 us (2%)
  other arithmetic  11.1 us (2%)
    all_gather x1, blocking collectives, local(): lax.all_gather(control_points, ('slab', 'ctrl'), axis=1, tiled=True)  229 us
    dot_general x16, matrix products, accumulate(): jnp.einsum('lnj,clj->cln', kernel, coeffs, precision=lax.Precision.HIGHEST)  170 us
    psum x1, blocking collectives, local(): total_loads = lax.psum(local_loads, ('slab', 'ctrl'))  107 us
    all_to_all x1, starting transfers between devices, local(): lax.all_to_all(jnp.stack([control_modes] * lax.axis_size(('slab', 'ctrl')...  23.3 us
    unnamed x26, local copies, waits for them, and re-layouts  12.9 us
  transfers between devices with their start and end apart: 3, of which 2 were waited for; matrix products, arithmetic and copies ran while one was open for 1% of the time, Pallas kernels for 0%

profile of v1, /device:TPU:4, one launch (start us, length us, event | category | flops | bytes accessed | tf_op | source)
XLA Modules:
  0.0 619.5 jit_solution(17119985288479074876)
XLA Ops:
  0.6 0.7 copy-done
  1.3 2.2 broadcast_bitcast_fusion
  3.6 5.5 reshape.187
  9.1 23.3 %all-to-all-start = ((f32[512,1,288]{2,1,0:T(1,128)}), f32[512,1,288]{2,1,0:T(1,128)S(1)}, u32[]{:S(2)}, u32[]{:S(2)}) async-start(f32[512,1,288]{2,1,0:T(1,128)} %reshape.187), calls=%async_computation | async-start | bytes 1572864 | tf_op jit(solution)/shard_map/all_to_all | solution.py:113
  32.6 0.7 subtract_reduce_fusion.2
  33.3 2.0 pad_maximum_fusion.4
  35.3 107.3 %psum.7 = f32[6]{0:T(128)S(1)} all-reduce(f32[6]{0:T(128)S(1)} %pad_maximum_fusion.4), channel_id=1, replica_groups=mesh['slab'=128,'ctrl'=4] {'slab','ctrl'}, use_global_device_ids=true, to_apply=%region_5.0 | all-reduce | flops 6 | bytes 48 | tf_op jit(solution)/shard_map/psum | solution.py:119
  142.6 229.4 %all-gather = f32[512,16,3]{1,2,0:T(4,128)S(1)} all-gather(f32[1,16,3]{1,2,0:T(4,128)S(1)} %bitcast.100), channel_id=1, replica_groups=mesh['slab'=128,'ctrl'=4] {'slab','ctrl'}, dimensions={0}, use_global_device_ids=true | all-gather | bytes 98496 | tf_op jit(solution)/shard_map/all_gather | solution.py:111
  374.5 2.6 reduce.4
  377.2 4.0 reshape.188
  381.1 4.5 bitcast_bitcast_fusion
  385.6 6.6 %copy.24 = f32[18,512,16]{2,1,0:T(8,128)} copy(f32[18,512,16]{0,2,1:T(8,128)} %bitcast_bitcast_fusion) | data formatting | bytes 1179648 | tf_op jit(solution)/shard_map/reshape | solution.py:112
  392.3 4.6 reshape_reshape.3
  397.3 1.1 fusion.43
  398.5 207.5 %while.13 = (s32[]{:T(128)}, f32[3,64,128]{2,0,1:T(4,128)S(1)}, s32[]{:T(128)}, s32[64,16]{0,1:T(8,128)S(1)}, f32[3,64,128]{2,0,1:T(4,128)S(1)}, /*index=5*/s32[...) while((s32[]{:T(128)}, f32[3,64,128]{2,0,1:T(4,128)S(1)}, ...), condition=%wide.region_7.9_spmd, body=%wide.region_6.8_spmd.sunk | while | flops 54601224 | bytes 1480693 | solution.py:60
  400.8 10.6 %fusion.70 = f32[3,64,128]{2,0,1:T(4,128)S(1)} fusion(f32[3,64,128]{2,0,1:T(4,128)S(1)} %get-tuple-element.258, f32[64,128]{1,0:T(8,128)S(1)} %bitcast.97, f32[64,128]{1,0:T(8,128)S(1)} %get-tuple-element.239, f32[64,128]{1,0:T(8,128)S(1)} %bitcast.98, f32[64,128]{1,0:T(8,128)S(1)} %get-tuple-element.241, f32[64,128]{1,0:T(8,128)S(1)} %bitcast.96, ...), kind=kOutput, calls=%fused_computation.31.clone.1 | convolution fusion | flops 54575104 | bytes 491648 | tf_op jit(solution)/shard_map/while/body/lnj,clj->cln/dot_general | solution.py:57
  412.2 0.7 gather_fusion
  413.7 10.6 %fusion.70 = f32[3,64,128]{2,0,1:T(4,128)S(1)} fusion(f32[3,64,128]{2,0,1:T(4,128)S(1)} %get-tuple-element.258, f32[64,128]{1,0:T(8,128)S(1)} %bitcast.97, f32[64,128]{1,0:T(8,128)S(1)} %get-tuple-element.239, f32[64,128]{1,0:T(8,128)S(1)} %bitcast.98, f32[64,128]{1,0:T(8,128)S(1)} %get-tuple-element.241, f32[64,128]{1,0:T(8,128)S(1)} %bitcast.96, ...), kind=kOutput, calls=%fused_computation.31.clone.1 | convolution fusion | flops 54575104 | bytes 491648 | tf_op jit(solution)/shard_map/while/body/lnj,clj->cln/dot_general | solution.py:57
  426.7 10.6 %fusion.70 = f32[3,64,128]{2,0,1:T(4,128)S(1)} fusion(f32[3,64,128]{2,0,1:T(4,128)S(1)} %get-tuple-element.258, f32[64,128]{1,0:T(8,128)S(1)} %bitcast.97, f32[64,128]{1,0:T(8,128)S(1)} %get-tuple-element.239, f32[64,128]{1,0:T(8,128)S(1)} %bitcast.98, f32[64,128]{1,0:T(8,128)S(1)} %get-tuple-element.241, f32[64,128]{1,0:T(8,128)S(1)} %bitcast.96, ...), kind=kOutput, calls=%fused_computation.31.clone.1 | convolution fusion | flops 54575104 | bytes 491648 | tf_op jit(solution)/shard_map/while/body/lnj,clj->cln/dot_general | solution.py:57
  438.0 0.7 gather_fusion
  438.9 0.7 gather_fusion.1
  439.6 10.6 %fusion.70 = f32[3,64,128]{2,0,1:T(4,128)S(1)} fusion(f32[3,64,128]{2,0,1:T(4,128)S(1)} %get-tuple-element.258, f32[64,128]{1,0:T(8,128)S(1)} %bitcast.97, f32[64,128]{1,0:T(8,128)S(1)} %get-tuple-element.239, f32[64,128]{1,0:T(8,128)S(1)} %bitcast.98, f32[64,128]{1,0:T(8,128)S(1)} %get-tuple-element.241, f32[64,128]{1,0:T(8,128)S(1)} %bitcast.96, ...), kind=kOutput, calls=%fused_computation.31.clone.1 | convolution fusion | flops 54575104 | bytes 491648 | tf_op jit(solution)/shard_map/while/body/lnj,clj->cln/dot_general | solution.py:57
  452.5 10.6 %fusion.70 = f32[3,64,128]{2,0,1:T(4,128)S(1)} fusion(f32[3,64,128]{2,0,1:T(4,128)S(1)} %get-tuple-element.258, f32[64,128]{1,0:T(8,128)S(1)} %bitcast.97, f32[64,128]{1,0:T(8,128)S(1)} %get-tuple-element.239, f32[64,128]{1,0:T(8,128)S(1)} %bitcast.98, f32[64,128]{1,0:T(8,128)S(1)} %get-tuple-element.241, f32[64,128]{1,0:T(8,128)S(1)} %bitcast.96, ...), kind=kOutput, calls=%fused_computation.31.clone.1 | convolution fusion | flops 54575104 | bytes 491648 | tf_op jit(solution)/shard_map/while/body/lnj,clj->cln/dot_general | solution.py:57
  463.9 0.7 gather_fusion
  464.8 0.7 gather_fusion.1
  465.5 10.6 %fusion.70 = f32[3,64,128]{2,0,1:T(4,128)S(1)} fusion(f32[3,64,128]{2,0,1:T(4,128)S(1)} %get-tuple-element.258, f32[64,128]{1,0:T(8,128)S(1)} %bitcast.97, f32[64,128]{1,0:T(8,128)S(1)} %get-tuple-element.239, f32[64,128]{1,0:T(8,128)S(1)} %bitcast.98, f32[64,128]{1,0:T(8,128)S(1)} %get-tuple-element.241, f32[64,128]{1,0:T(8,128)S(1)} %bitcast.96, ...), kind=kOutput, calls=%fused_computation.31.clone.1 | convolution fusion | flops 54575104 | bytes 491648 | tf_op jit(solution)/shard_map/while/body/lnj,clj->cln/dot_general | solution.py:57
  478.4 10.6 %fusion.70 = f32[3,64,128]{2,0,1:T(4,128)S(1)} fusion(f32[3,64,128]{2,0,1:T(4,128)S(1)} %get-tuple-element.258, f32[64,128]{1,0:T(8,128)S(1)} %bitcast.97, f32[64,128]{1,0:T(8,128)S(1)} %get-tuple-element.239, f32[64,128]{1,0:T(8,128)S(1)} %bitcast.98, f32[64,128]{1,0:T(8,128)S(1)} %get-tuple-element.241, f32[64,128]{1,0:T(8,128)S(1)} %bitcast.96, ...), kind=kOutput, calls=%fused_computation.31.clone.1 | convolution fusion | flops 54575104 | bytes 491648 | tf_op jit(solution)/shard_map/while/body/lnj,clj->cln/dot_general | solution.py:57
  489.8 0.7 gather_fusion
  490.7 0.7 gather_fusion.1
  491.3 10.6 %fusion.70 = f32[3,64,128]{2,0,1:T(4,128)S(1)} fusion(f32[3,64,128]{2,0,1:T(4,128)S(1)} %get-tuple-element.258, f32[64,128]{1,0:T(8,128)S(1)} %bitcast.97, f32[64,128]{1,0:T(8,128)S(1)} %get-tuple-element.239, f32[64,128]{1,0:T(8,128)S(1)} %bitcast.98, f32[64,128]{1,0:T(8,128)S(1)} %get-tuple-element.241, f32[64,128]{1,0:T(8,128)S(1)} %bitcast.96, ...), kind=kOutput, calls=%fused_computation.31.clone.1 | convolution fusion | flops 54575104 | bytes 491648 | tf_op jit(solution)/shard_map/while/body/lnj,clj->cln/dot_general | solution.py:57
  504.3 10.6 %fusion.70 = f32[3,64,128]{2,0,1:T(4,128)S(1)} fusion(f32[3,64,128]{2,0,1:T(4,128)S(1)} %get-tuple-element.258, f32[64,128]{1,0:T(8,128)S(1)} %bitcast.97, f32[64,128]{1,0:T(8,128)S(1)} %get-tuple-element.239, f32[64,128]{1,0:T(8,128)S(1)} %bitcast.98, f32[64,128]{1,0:T(8,128)S(1)} %get-tuple-element.241, f32[64,128]{1,0:T(8,128)S(1)} %bitcast.96, ...), kind=kOutput, calls=%fused_computation.31.clone.1 | convolution fusion | flops 54575104 | bytes 491648 | tf_op jit(solution)/shard_map/while/body/lnj,clj->cln/dot_general | solution.py:57
  517.2 10.6 %fusion.70 = f32[3,64,128]{2,0,1:T(4,128)S(1)} fusion(f32[3,64,128]{2,0,1:T(4,128)S(1)} %get-tuple-element.258, f32[64,128]{1,0:T(8,128)S(1)} %bitcast.97, f32[64,128]{1,0:T(8,128)S(1)} %get-tuple-element.239, f32[64,128]{1,0:T(8,128)S(1)} %bitcast.98, f32[64,128]{1,0:T(8,128)S(1)} %get-tuple-element.241, f32[64,128]{1,0:T(8,128)S(1)} %bitcast.96, ...), kind=kOutput, calls=%fused_computation.31.clone.1 | convolution fusion | flops 54575104 | bytes 491648 | tf_op jit(solution)/shard_map/while/body/lnj,clj->cln/dot_general | solution.py:57
  530.1 10.6 %fusion.70 = f32[3,64,128]{2,0,1:T(4,128)S(1)} fusion(f32[3,64,128]{2,0,1:T(4,128)S(1)} %get-tuple-element.258, f32[64,128]{1,0:T(8,128)S(1)} %bitcast.97, f32[64,128]{1,0:T(8,128)S(1)} %get-tuple-element.239, f32[64,128]{1,0:T(8,128)S(1)} %bitcast.98, f32[64,128]{1,0:T(8,128)S(1)} %get-tuple-element.241, f32[64,128]{1,0:T(8,128)S(1)} %bitcast.96, ...), kind=kOutput, calls=%fused_computation.31.clone.1 | convolution fusion | flops 54575104 | bytes 491648 | tf_op jit(solution)/shard_map/while/body/lnj,clj->cln/dot_general | solution.py:57
  541.5 0.7 gather_fusion
  542.4 0.7 gather_fusion.1
  543.1 10.6 %fusion.70 = f32[3,64,128]{2,0,1:T(4,128)S(1)} fusion(f32[3,64,128]{2,0,1:T(4,128)S(1)} %get-tuple-element.258, f32[64,128]{1,0:T(8,128)S(1)} %bitcast.97, f32[64,128]{1,0:T(8,128)S(1)} %get-tuple-element.239, f32[64,128]{1,0:T(8,128)S(1)} %bitcast.98, f32[64,128]{1,0:T(8,128)S(1)} %get-tuple-element.241, f32[64,128]{1,0:T(8,128)S(1)} %bitcast.96, ...), kind=kOutput, calls=%fused_computation.31.clone.1 | convolution fusion | flops 54575104 | bytes 491648 | tf_op jit(solution)/shard_map/while/body/lnj,clj->cln/dot_general | solution.py:57
  554.4 0.7 gather_fusion
  555.3 0.7 gather_fusion.1
  556.0 10.6 %fusion.70 = f32[3,64,128]{2,0,1:T(4,128)S(1)} fusion(f32[3,64,128]{2,0,1:T(4,128)S(1)} %get-tuple-element.258, f32[64,128]{1,0:T(8,128)S(1)} %bitcast.97, f32[64,128]{1,0:T(8,128)S(1)} %get-tuple-element.239, f32[64,128]{1,0:T(8,128)S(1)} %bitcast.98, f32[64,128]{1,0:T(8,128)S(1)} %get-tuple-element.241, f32[64,128]{1,0:T(8,128)S(1)} %bitcast.96, ...), kind=kOutput, calls=%fused_computation.31.clone.1 | convolution fusion | flops 54575104 | bytes 491648 | tf_op jit(solution)/shard_map/while/body/lnj,clj->cln/dot_general | solution.py:57
  568.9 10.6 %fusion.70 = f32[3,64,128]{2,0,1:T(4,128)S(1)} fusion(f32[3,64,128]{2,0,1:T(4,128)S(1)} %get-tuple-element.258, f32[64,128]{1,0:T(8,128)S(1)} %bitcast.97, f32[64,128]{1,0:T(8,128)S(1)} %get-tuple-element.239, f32[64,128]{1,0:T(8,128)S(1)} %bitcast.98, f32[64,128]{1,0:T(8,128)S(1)} %get-tuple-element.241, f32[64,128]{1,0:T(8,128)S(1)} %bitcast.96, ...), kind=kOutput, calls=%fused_computation.31.clone.1 | convolution fusion | flops 54575104 | bytes 491648 | tf_op jit(solution)/shard_map/while/body/lnj,clj->cln/dot_general | solution.py:57
  580.3 0.7 gather_fusion
  581.2 0.7 gather_fusion.1
  581.9 10.6 %fusion.70 = f32[3,64,128]{2,0,1:T(4,128)S(1)} fusion(f32[3,64,128]{2,0,1:T(4,128)S(1)} %get-tuple-element.258, f32[64,128]{1,0:T(8,128)S(1)} %bitcast.97, f32[64,128]{1,0:T(8,128)S(1)} %get-tuple-element.239, f32[64,128]{1,0:T(8,128)S(1)} %bitcast.98, f32[64,128]{1,0:T(8,128)S(1)} %get-tuple-element.241, f32[64,128]{1,0:T(8,128)S(1)} %bitcast.96, ...), kind=kOutput, calls=%fused_computation.31.clone.1 | convolution fusion | flops 54575104 | bytes 491648 | tf_op jit(solution)/shard_map/while/body/lnj,clj->cln/dot_general | solution.py:57
  594.8 10.6 %fusion.70 = f32[3,64,128]{2,0,1:T(4,128)S(1)} fusion(f32[3,64,128]{2,0,1:T(4,128)S(1)} %get-tuple-element.258, f32[64,128]{1,0:T(8,128)S(1)} %bitcast.97, f32[64,128]{1,0:T(8,128)S(1)} %get-tuple-element.239, f32[64,128]{1,0:T(8,128)S(1)} %bitcast.98, f32[64,128]{1,0:T(8,128)S(1)} %get-tuple-element.241, f32[64,128]{1,0:T(8,128)S(1)} %bitcast.96, ...), kind=kOutput, calls=%fused_computation.31.clone.1 | convolution fusion | flops 54575104 | bytes 491648 | tf_op jit(solution)/shard_map/while/body/lnj,clj->cln/dot_general | solution.py:57
  606.8 4.3 collective-permute-start
  611.1 1.4 collective-permute-done
  612.5 1.3 collective-permute-start.1
  614.0 4.3 collective-permute-done.1
  (148 shorter events, 21.5 us)
Async XLA Ops:
  0.6 0.7 copy-start
  3.5 28.9 %copy-start.2 = (f32[3,4096]{1,0:T(4,128)S(1)}, f32[3,4096]{1,0:T(4,128)}, u32[]{:S(2)}) copy-start(f32[3,4096]{1,0:T(4,128)} %param.16) | copy-start | bytes 147460
  3.5 28.9 %copy-start.5 = (f32[4096]{0:T(1024)S(1)}, f32[4096]{0:T(1024)}, u32[]{:S(2)}) copy-start(f32[4096]{0:T(1024)} %param.15) | copy-start | bytes 49156
  3.5 29.0 %copy-start.3 = (f32[3,4096]{1,0:T(4,128)S(1)}, f32[3,4096]{1,0:T(4,128)}, u32[]{:S(2)}) copy-start(f32[3,4096]{1,0:T(4,128)} %param.17) | copy-start | bytes 147460
  3.5 139.1 %copy-start.10 = (f32[3,16]{1,0:T(4,128)S(1)}, f32[3,16]{1,0:T(4,128)}, u32[]{:S(2)}) copy-start(f32[3,16]{1,0:T(4,128)} %param.20) | copy-start | bytes 580
  3.5 369.0 %copy-start.4 = (s32[8,8,16]{2,1,0:T(8,128)S(1)}, s32[8,8,16]{2,1,0:T(8,128)}, u32[]{:S(2)}) copy-start(s32[8,8,16]{2,1,0:T(8,128)} %param.23) | copy-start | bytes 12292
  3.6 369.0 %copy-start.6 = (s32[8,8]{1,0:T(8,128)S(1)}, s32[8,8]{1,0:T(8,128)}, u32[]{:S(2)}) copy-start(s32[8,8]{1,0:T(8,128)} %param.24) | copy-start | bytes 772
  3.6 369.8 %copy-start.7 = (f32[6]{0:T(128)S(1)}, f32[6]{0:T(128)}, u32[]{:S(2)}) copy-start(f32[6]{0:T(128)} %param.18) | copy-start | bytes 76
  3.6 369.8 %copy-start.8 = (f32[6]{0:T(128)S(1)}, f32[6]{0:T(128)}, u32[]{:S(2)}) copy-start(f32[6]{0:T(128)} %param.19) | copy-start | bytes 76
  3.6 369.8 %copy-start.9 = (f32[6]{0:T(128)S(1)}, f32[6]{0:T(128)}, u32[]{:S(2)}) copy-start(f32[6]{0:T(128)} %constant.102.clone) | copy-start | bytes 76
  9.1 364.9 %all-to-all-start = ((f32[512,1,288]{2,1,0:T(1,128)}), f32[512,1,288]{2,1,0:T(1,128)S(1)}, u32[]{:S(2)}, u32[]{:S(2)}) async-start(f32[512,1,288]{2,1,0:T(1,128)} %reshape.187), calls=%async_computation | async-start | bytes 1572864 | tf_op jit(solution)/shard_map/all_to_all | solution.py:113
  392.3 6.3 %copy-start.1 = (f32[3,8,8,128]{3,2,1,0:T(8,128)S(1)}, f32[3,8,8,128]{3,2,1,0:T(8,128)}, u32[]{:S(2)}) copy-start(f32[3,8,8,128]{3,2,1,0:T(8,128)} %param.22) | copy-start | bytes 294916
  606.8 5.8 collective-permute-start
  612.5 5.8 collective-permute-start.1
